TPU v7x, 32 devices: a whole 2x2x4 slice. The times are simulated.
32 devices in a mesh: fsdp: 16 (over z, y, core), seq: 2 (over x).
Axes of the slice: x: 2, y: 2, z: 4, core: 2. Of those that a mesh axis runs over, the one named last changes fastest.
Arguments:
- stream: bfloat16 [6144, 1024], P(('fsdp', 'seq')), may hold values from -6 to 6
- cotangent: bfloat16 [6144, 1024], P(('fsdp', 'seq')), may hold values from -6 to 6
- doc_lengths: int32 [10], replicated, may hold values from 1 to 1153, 6144 in all
- attention_gain: bfloat16 [1024], P('fsdp'), may hold values from 0.5 to 1.5
- query_weight: bfloat16 [1024, 1024], P('fsdp'), may hold values from -0.1875 to 0.1875
- key_matrix: bfloat16 [1024, 512], P('fsdp'), may hold values from -0.1875 to 0.1875
- value_matrix: bfloat16 [1024, 512], P('fsdp'), may hold values from -0.1875 to 0.1875
- query_gain: bfloat16 [64], P('fsdp'), may hold values from 0.5 to 1.5
- key_gain: bfloat16 [64], P('fsdp'), may hold values from 0.5 to 1.5
- output_weight: bfloat16 [1024, 1024], P('fsdp'), may hold values from -3 to 3
- feedforward_gain: bfloat16 [1024], P('fsdp'), may hold values from 0.5 to 1.5
- gate_weight: bfloat16 [1024, 4608], P('fsdp'), may hold values from -0.1875 to 0.1875
- up_weight: bfloat16 [1024, 4608], P('fsdp'), may hold values from -0.1875 to 0.1875
- down_weight: bfloat16 [4608, 1024], P('fsdp'), may hold values from -0.09375 to 0.09375
Outputs:
- result: bfloat16 [6144, 1024], P(('fsdp', 'seq'))
- grad_stream: bfloat16 [6144, 1024], P(('fsdp', 'seq'))
- grad_attention_gain: float32 [1024], P('fsdp')
- grad_query: float32 [1024, 1024], P('fsdp')
- grad_key: float32 [1024, 512], P('fsdp')
- grad_value: float32 [1024, 512], P('fsdp')
- grad_query_gain: float32 [64], P('fsdp')
- grad_key_gain: float32 [64], P('fsdp')
- grad_output: float32 [1024, 1024], P('fsdp')
- grad_feedforward_gain: float32 [1024], P('fsdp')
- grad_gate: float32 [1024, 4608], P('fsdp')
- grad_up: float32 [1024, 4608], P('fsdp')
- grad_down: float32 [4608, 1024], P('fsdp')
Inputs may be any that keep to these rules, and one draw needn't show every extreme that they name: `doc_lengths`: they sum to 6144, and the longest has exactly 1153 tokens.
All inputs are finite; a program needn't handle non-finite values.
Results may differ from a plain program's by a relative error of at most 0.03.
Values may be sent and summed in bfloat16 or wider, within the bound.
No kernel may reach another device: no remote copies, remote signals or barrier semaphores. Data moves between devices by JAX's collectives and lax.ppermute only.
A program may use at most 192 MiB of HBM per device.

v0:
```python
import math
import jax
import jax.numpy as jnp
from jax import lax
from jax.sharding import PartitionSpec as P

QUERY_HEAD_COUNT = 16
KEY_VALUE_HEADS = 8
HEAD_SIZE = 64
DOC_MIN = 1024
EPS = 1e-05
THETA = 1000000.0
NEGATIVE = -1e30


def shifted(value, axis, steps):
    count = lax.axis_size(axis)
    first, last = (max(0, -steps), min(count, count - steps))
    return lax.ppermute(value, axis, [(source, source + steps) for source in range(first, last)])


def product(left, right):
    return jnp.dot(left, right, preferred_element_type=jnp.float32)


def product_left(left, right):
    return lax.dot_general(
        left, right, (((0,), (0,)), ((), ())), preferred_element_type=jnp.float32
    )


def product_right(left, right):
    return lax.dot_general(
        left, right, (((1,), (1,)), ((), ())), preferred_element_type=jnp.float32
    )


def doc_start(starts, places):
    inside = starts[None, :] <= places[:, None]
    return jnp.max(jnp.where(inside, starts[None, :], -1), axis=1)


def rotate(values, start_offset):
    half = values.shape[-1] // 2
    ladder = jnp.arange(half, dtype=jnp.float32) * (2.0 / values.shape[-1])
    freq = jnp.power(THETA, -ladder)
    angle = start_offset.astype(jnp.float32)[:, None] * freq[None, :]
    cosine = jnp.cos(angle)[:, None, :]
    sine = jnp.sin(angle)[:, None, :]
    front = values[..., :half]
    behind = values[..., half:]
    return jnp.concatenate(
        [front * cosine - behind * sine, behind * cosine + front * sine], axis=-1
    )


def prepare_heads(linear_map, norm_gain, start_offset, heads):
    count = linear_map.shape[0]
    split = linear_map.reshape(count, heads, -1)
    normed = split * lax.rsqrt(jnp.mean(split * split, axis=-1, keepdims=True) + EPS) * norm_gain
    return rotate(normed, start_offset).reshape(count, -1)


def norm_forward(values, norm_gain):
    factor = lax.rsqrt(jnp.mean(values * values, axis=-1, keepdims=True) + EPS)
    normed = values * factor
    return (normed * norm_gain, normed, factor)


def norm_backward(grad, normed, factor, norm_gain):
    gain_grad = jnp.sum(grad * normed, axis=0)
    scaled = grad * norm_gain
    return (
        factor * (scaled - normed * jnp.mean(scaled * normed, axis=-1, keepdims=True)),
        gain_grad,
    )


def on_device(
    stream,
    cotangent,
    doc_lengths,
    attention_gain,
    query_weight,
    key_matrix,
    value_matrix,
    query_gain,
    key_gain,
    output_weight,
    feedforward_gain,
    gate_weight,
    up_weight,
    down_weight,
):
    rows = stream.shape[0]
    sequence_count = lax.axis_size("seq")
    shard_index = lax.axis_index("fsdp")
    seq_index = lax.axis_index("seq")
    block = rows * sequence_count
    lookback = max(2, -(-DOC_MIN // block))
    group_size = QUERY_HEAD_COUNT // KEY_VALUE_HEADS
    local_key_value = KEY_VALUE_HEADS // sequence_count
    scale = HEAD_SIZE ** (-0.5)
    query_row_count = math.gcd(512, block)
    blocks_q = block // query_row_count
    starts = jnp.cumsum(doc_lengths) - doc_lengths
    places = (shard_index * sequence_count + seq_index) * rows + jnp.arange(rows, dtype=jnp.int32)
    start_offset = places - doc_start(starts, places)
    query_place = shard_index * block + jnp.arange(block, dtype=jnp.int32)
    query_start = doc_start(starts, query_place)
    key_place = jnp.concatenate(
        [
            (shard_index - step) * block + jnp.arange(block, dtype=jnp.int32)
            for step in range(lookback + 1)
        ]
    )
    key_start = doc_start(starts, key_place)
    gathered = (
        lax.all_gather(attention_gain, "fsdp", axis=0, tiled=True),
        lax.all_gather(query_weight, "fsdp", axis=0, tiled=True),
        lax.all_gather(key_matrix, "fsdp", axis=0, tiled=True),
        lax.all_gather(value_matrix, "fsdp", axis=0, tiled=True),
        lax.all_gather(query_gain, "fsdp", axis=0, tiled=True),
        lax.all_gather(key_gain, "fsdp", axis=0, tiled=True),
        lax.all_gather(output_weight, "fsdp", axis=0, tiled=True),
        lax.all_gather(feedforward_gain, "fsdp", axis=0, tiled=True),
        lax.all_gather(gate_weight, "fsdp", axis=0, tiled=True),
        lax.all_gather(up_weight, "fsdp", axis=0, tiled=True),
        lax.all_gather(down_weight, "fsdp", axis=0, tiled=True),
    )
    gain_one = gathered[0].astype(jnp.float32)
    full_query = gathered[1]
    full_key = gathered[2]
    full_value = gathered[3]
    gain_query = gathered[4].astype(jnp.float32)
    gain_key = gathered[5].astype(jnp.float32)
    full_output = gathered[6]
    gain_two = gathered[7].astype(jnp.float32)
    full_gate = gathered[8]
    full_up = gathered[9]
    full_down = gathered[10]
    inputs = stream.astype(jnp.float32)
    normed_one, plain_one, factor_one = norm_forward(inputs, gain_one)
    hidden = normed_one.astype(jnp.bfloat16)
    query_lin = product(hidden, full_query)
    key_linear = product(hidden, full_key)
    value_lin = product(hidden, full_value)

    def prep_query(linear_map, norm_gain):
        return prepare_heads(linear_map, norm_gain, start_offset, QUERY_HEAD_COUNT)

    def prep_key(linear_map, norm_gain):
        return prepare_heads(linear_map, norm_gain, start_offset, KEY_VALUE_HEADS)

    query_rot, query_pull = jax.vjp(prep_query, query_lin, gain_query)
    key_rot, key_pull = jax.vjp(prep_key, key_linear, gain_key)
    query_heads, key_heads, value_heads = (
        lax.all_to_all(
            query_rot.astype(jnp.bfloat16), "seq", split_axis=1, concat_axis=0, tiled=True
        ),
        lax.all_to_all(
            key_rot.astype(jnp.bfloat16), "seq", split_axis=1, concat_axis=0, tiled=True
        ),
        lax.all_to_all(
            value_lin.astype(jnp.bfloat16), "seq", split_axis=1, concat_axis=0, tiled=True
        ),
    )
    key_pair = jnp.stack([key_heads, value_heads])
    pairs = [key_pair]
    moving = key_pair
    for step in range(lookback):
        moving = shifted(moving, "fsdp", 1)
        pairs.append(moving)
    all_keys = jnp.concatenate([pair[0] for pair in pairs]).reshape(-1, local_key_value, HEAD_SIZE)
    all_values = jnp.concatenate([pair[1] for pair in pairs]).reshape(
        -1, local_key_value, HEAD_SIZE
    )
    query_split = query_heads.reshape(
        blocks_q, query_row_count, local_key_value, group_size, HEAD_SIZE
    )
    start_split = query_start.reshape(blocks_q, query_row_count)
    place_split = query_place.reshape(blocks_q, query_row_count)

    def scores_of(query_tile, start_block, place_block):
        score = (
            jnp.einsum("qhgd,khd->hgqk", query_tile, all_keys, preferred_element_type=jnp.float32)
            * scale
        )
        allowed = (key_start[None, :] == start_block[:, None]) & (
            key_place[None, :] <= place_block[:, None]
        )
        return jnp.where(allowed, score, NEGATIVE)

    def attend(items):
        query_tile, start_block, place_block = items
        score = scores_of(query_tile, start_block, place_block)
        highest = jnp.max(score, axis=-1, keepdims=True)
        weight = jnp.exp(score - highest)
        total = jnp.sum(weight, axis=-1, keepdims=True)
        mixed = jnp.einsum(
            "hgqk,khd->qhgd",
            (weight / total).astype(jnp.bfloat16),
            all_values,
            preferred_element_type=jnp.float32,
        )
        return (
            mixed.reshape(query_row_count, -1).astype(jnp.bfloat16),
            (highest + jnp.log(total))[..., 0],
        )

    mixed_heads, log_total = lax.map(attend, (query_split, start_split, place_split))
    attended = lax.all_to_all(
        mixed_heads.reshape(block, -1), "seq", split_axis=0, concat_axis=1, tiled=True
    )
    middle = inputs + product(attended, full_output)
    normed_two, plain_two, factor_two = norm_forward(middle, gain_two)
    hidden_two = normed_two.astype(jnp.bfloat16)
    gate = product(hidden_two, full_gate)
    upward = product(hidden_two, full_up)
    inner = (jax.nn.silu(gate) * upward).astype(jnp.bfloat16)
    result = (middle + product(inner, full_down)).astype(jnp.bfloat16)
    d_inner = product_right(cotangent, full_down)
    sigma = jax.nn.sigmoid(gate)
    d_gate = (d_inner * upward * sigma * (1.0 + gate * (1.0 - sigma))).astype(jnp.bfloat16)
    d_up = (d_inner * gate * sigma).astype(jnp.bfloat16)
    d_two = product_right(d_gate, full_gate) + product_right(d_up, full_up)
    d_norm_two, grad_gain_two = norm_backward(d_two, plain_two, factor_two, gain_two)
    d_middle = cotangent.astype(jnp.float32) + d_norm_two
    d_mid = d_middle.astype(jnp.bfloat16)
    d_attended = product_right(d_mid, full_output).astype(jnp.bfloat16)
    d_heads = lax.all_to_all(d_attended, "seq", split_axis=1, concat_axis=0, tiled=True)
    d_split = d_heads.reshape(blocks_q, query_row_count, local_key_value, group_size, HEAD_SIZE)

    def attend_back(carry, items):
        d_keys, d_values = carry
        query_tile, start_block, place_block, d_block, total_block = items
        score = scores_of(query_tile, start_block, place_block)
        prob = jnp.exp(score - total_block[..., None])
        d_prob = jnp.einsum(
            "qhgd,khd->hgqk", d_block, all_values, preferred_element_type=jnp.float32
        )
        row_sum = jnp.sum(prob * d_prob, axis=-1, keepdims=True)
        d_score = (prob * (d_prob - row_sum)).astype(jnp.bfloat16)
        d_query = (
            jnp.einsum("hgqk,khd->qhgd", d_score, all_keys, preferred_element_type=jnp.float32)
            * scale
        )
        d_keys = (
            d_keys
            + jnp.einsum("hgqk,qhgd->khd", d_score, query_tile, preferred_element_type=jnp.float32)
            * scale
        )
        d_values = d_values + jnp.einsum(
            "hgqk,qhgd->khd", prob.astype(jnp.bfloat16), d_block, preferred_element_type=jnp.float32
        )
        return ((d_keys, d_values), d_query.reshape(query_row_count, -1).astype(jnp.bfloat16))

    empty = jnp.zeros(all_keys.shape, jnp.float32)
    (d_keys, d_values), d_queries = lax.scan(
        attend_back, (empty, empty), (query_split, start_split, place_split, d_split, log_total)
    )
    key_parts = d_keys.reshape(lookback + 1, block, local_key_value * HEAD_SIZE)
    value_parts = d_values.reshape(lookback + 1, block, local_key_value * HEAD_SIZE)
    parts = [jnp.stack([key_parts[step], value_parts[step]]) for step in range(lookback + 1)]
    d_pair = parts[lookback]
    for step in range(lookback, 0, -1):
        d_pair = (
            shifted(d_pair.astype(jnp.bfloat16), "fsdp", -1).astype(d_pair.dtype) + parts[step - 1]
        )
    d_query_tok, d_key_tok, d_value_tok = (
        lax.all_to_all(
            d_queries.reshape(block, -1), "seq", split_axis=0, concat_axis=1, tiled=True
        ),
        lax.all_to_all(
            d_pair[0].astype(jnp.bfloat16), "seq", split_axis=0, concat_axis=1, tiled=True
        ),
        lax.all_to_all(
            d_pair[1].astype(jnp.bfloat16), "seq", split_axis=0, concat_axis=1, tiled=True
        ),
    )
    d_query_lin, grad_query_gain = query_pull(d_query_tok.astype(jnp.float32))
    d_key_lin, grad_key_gain = key_pull(d_key_tok.astype(jnp.float32))
    d_query_low = d_query_lin.astype(jnp.bfloat16)
    d_key_low = d_key_lin.astype(jnp.bfloat16)
    d_hidden = (
        product_right(d_query_low, full_query)
        + product_right(d_key_low, full_key)
        + product_right(d_value_tok, full_value)
    )
    d_norm_one, grad_gain_one = norm_backward(d_hidden, plain_one, factor_one, gain_one)
    grad_stream = (d_middle + d_norm_one).astype(jnp.bfloat16)
    grad_down = product_left(inner, cotangent)
    grad_gate = product_left(hidden_two, d_gate)
    grad_up = product_left(hidden_two, d_up)
    grad_output = product_left(attended, d_mid)
    grad_query = product_left(hidden, d_query_low)
    grad_key = product_left(hidden, d_key_low)
    grad_value = product_left(hidden, d_value_tok)
    shards = (
        lax.psum_scatter(
            grad_gain_one.astype(jnp.bfloat16), "fsdp", scatter_dimension=0, tiled=True
        ).astype(jnp.float32),
        lax.psum_scatter(
            grad_query.astype(jnp.bfloat16), "fsdp", scatter_dimension=0, tiled=True
        ).astype(jnp.float32),
        lax.psum_scatter(
            grad_key.astype(jnp.bfloat16), "fsdp", scatter_dimension=0, tiled=True
        ).astype(jnp.float32),
        lax.psum_scatter(
            grad_value.astype(jnp.bfloat16), "fsdp", scatter_dimension=0, tiled=True
        ).astype(jnp.float32),
        lax.psum_scatter(
            grad_query_gain.astype(jnp.bfloat16), "fsdp", scatter_dimension=0, tiled=True
        ).astype(jnp.float32),
        lax.psum_scatter(
            grad_key_gain.astype(jnp.bfloat16), "fsdp", scatter_dimension=0, tiled=True
        ).astype(jnp.float32),
        lax.psum_scatter(
            grad_output.astype(jnp.bfloat16), "fsdp", scatter_dimension=0, tiled=True
        ).astype(jnp.float32),
        lax.psum_scatter(
            grad_gain_two.astype(jnp.bfloat16), "fsdp", scatter_dimension=0, tiled=True
        ).astype(jnp.float32),
        lax.psum_scatter(
            grad_gate.astype(jnp.bfloat16), "fsdp", scatter_dimension=0, tiled=True
        ).astype(jnp.float32),
        lax.psum_scatter(
            grad_up.astype(jnp.bfloat16), "fsdp", scatter_dimension=0, tiled=True
        ).astype(jnp.float32),
        lax.psum_scatter(
            grad_down.astype(jnp.bfloat16), "fsdp", scatter_dimension=0, tiled=True
        ).astype(jnp.float32),
    )
    totals = (
        lax.psum(shards[0].astype(jnp.bfloat16), "seq").astype(jnp.float32),
        lax.psum(shards[1].astype(jnp.bfloat16), "seq").astype(jnp.float32),
        lax.psum(shards[2].astype(jnp.bfloat16), "seq").astype(jnp.float32),
        lax.psum(shards[3].astype(jnp.bfloat16), "seq").astype(jnp.float32),
        lax.psum(shards[4].astype(jnp.bfloat16), "seq").astype(jnp.float32),
        lax.psum(shards[5].astype(jnp.bfloat16), "seq").astype(jnp.float32),
        lax.psum(shards[6].astype(jnp.bfloat16), "seq").astype(jnp.float32),
        lax.psum(shards[7].astype(jnp.bfloat16), "seq").astype(jnp.float32),
        lax.psum(shards[8].astype(jnp.bfloat16), "seq").astype(jnp.float32),
        lax.psum(shards[9].astype(jnp.bfloat16), "seq").astype(jnp.float32),
        lax.psum(shards[10].astype(jnp.bfloat16), "seq").astype(jnp.float32),
    )
    outputs = (
        totals[0],
        totals[1],
        totals[2],
        totals[3],
        totals[4],
        totals[5],
        totals[6],
        totals[7],
        totals[8],
        totals[9],
        totals[10],
    )
    return (result, grad_stream) + outputs


def solution(mesh):
    placed = (
        P(("fsdp", "seq"), None),
        P(("fsdp", "seq"), None),
        P(),
        P("fsdp"),
        P("fsdp", None),
        P("fsdp", None),
        P("fsdp", None),
        P("fsdp"),
        P("fsdp"),
        P("fsdp", None),
        P("fsdp"),
        P("fsdp", None),
        P("fsdp", None),
        P("fsdp", None),
    )
    return jax.shard_map(
        on_device,
        mesh=mesh,
        in_specs=placed,
        out_specs=(
            P(("fsdp", "seq"), None),
            P(("fsdp", "seq"), None),
            P("fsdp"),
            P("fsdp", None),
            P("fsdp", None),
            P("fsdp", None),
            P("fsdp"),
            P("fsdp"),
            P("fsdp", None),
            P("fsdp"),
            P("fsdp", None),
            P("fsdp", None),
            P("fsdp", None),
        ),
        check_vma=False,
    )
```

profile of v0, /device:TPU:0, one launch (start us, length us, event | category | flops | bytes accessed | tf_op | source)
XLA Modules:
  0.0 1242.6 jit_solution(9412781983288827578)
XLA Ops:
  17.9 36.1 %all-reduce.13 = (bf16[64]{0:T(256)(128)(2,1)S(1)}, bf16[1024]{0:T(1024)(128)(2,1)S(1)}, bf16[64]{0:T(256)(128)(2,1)S(1)}, bf16[1024]{0:T(1024)(128)(2,1)}) all-reduce(bf16[64]{0:T(256)(128)(2,1)S(1)} %dynamic-update-slice.1, bf16[1024]{0:T(1024)(128)(2,1)S(1)} %dynamic-update-slice, ...), channel_id=1, replica_groups=mesh['fsdp'=16,'seq'=2] {'fsdp'}, use_global_device_ids=true, to_apply=%add.5 | all-reduce | flops 2176 | bytes 8704
  59.6 3.4 all-to-all-start.2
  63.0 27.1 %all-gather.10.cloned.1.call-done = bf16[1024,512]{1,0:T(8,128)(2,1)} async-done(((bf16[64,512]{1,0:T(8,128)(2,1)}), bf16[1024,512]{1,0:T(8,128)(2,1)}) %all-gather.10.cloned.1.call-update) | async-done | bytes 1048592 | tf_op jit(solution)/shard_map/all_gather | solution.py:121
  93.2 7.6 all_to_all.116
  103.4 6.5 collective-permute-start.1
  112.0 9.3 collective-permute-start.2
  123.5 10.6 all-gather.8.cloned.1.call-done
  134.1 2.6 multiply_reduce_fusion.2
  139.1 3.8 all-to-all-start
  144.2 5.9 all-to-all-done
  151.9 27.9 %while.27 = (s32[]{:T(128)}, bf16[3,128,512]{2,1,0:T(8,128)(2,1)}, f32[3,4,2,128]{3,2,1,0:T(2,128)}, s32[1536]{0:T(1024)S(1)}, s32[3,128]{1,0:T(4,128)}, /*index...) while((s32[]{:T(128)}, bf16[3,128,512]{2,1,0:T(8,128)(2,1)}, ...), condition=%wide.region_10.11_spmd, body=%wide.region_7.10_spmd.sunk | while | flops 422181888 | bytes 22068356 | solution.py:211
  152.9 2.4 bitcast_reduce_fusion.2
  156.9 3.0 fusion.147
  162.2 2.4 bitcast_reduce_fusion.2
  166.2 3.0 fusion.147
  171.5 2.4 bitcast_reduce_fusion.2
  175.5 3.0 fusion.147
  179.8 4.0 all-to-all-start.3
  183.9 6.4 all-to-all-done.3
  190.4 2.4 multiply_reduce_fusion.5
  192.9 65.6 %all-gather.16.cloned.1.call-done = bf16[1024,4608]{1,0:T(8,128)(2,1)} async-done(((bf16[64,4608]{1,0:T(8,128)(2,1)}), bf16[1024,4608]{1,0:T(8,128)(2,1)}) %all-gather.16.cloned.1.call-update) | async-done | bytes 9437200 | tf_op jit(solution)/shard_map/all_gather | solution.py:127
  258.5 7.5 fusion.85
  266.0 74.3 %all-gather.18.cloned.1.call-done = bf16[1024,4608]{1,0:T(8,128)(2,1)} async-done(((bf16[64,4608]{1,0:T(8,128)(2,1)}), bf16[1024,4608]{1,0:T(8,128)(2,1)}) %all-gather.18.cloned.1.call-update) | async-done | bytes 9437200 | tf_op jit(solution)/shard_map/all_gather | solution.py:128
  340.3 7.5 fusion.86
  347.7 74.4 %all-gather.20.cloned.1.call-done = bf16[4608,1024]{1,0:T(8,128)(2,1)} async-done(((bf16[288,1024]{1,0:T(8,128)(2,1)}), bf16[4608,1024]{1,0:T(8,128)(2,1)}) %all-gather.20.cloned.1.call-update) | async-done | bytes 9437200 | tf_op jit(solution)/shard_map/all_gather | solution.py:129
  422.2 11.2 multiply_convert_fusion
  433.4 8.2 fusion.87
  441.6 3.8 multiply_reduce_fusion.3
  448.7 3.5 all-to-all-start.4
  452.4 7.0 all-to-all-done.4
  462.3 63.8 %while.28 = (s32[]{:T(128)}, f32[1536,4,64]{0,2,1:T(8,128)}, f32[1536,4,64]{0,2,1:T(8,128)}, bf16[3,128,512]{2,1,0:T(8,128)(2,1)}, bf16[3,128,4,2,64]{1,4,3,2,0:...) while((s32[]{:T(128)}, f32[1536,4,64]{0,2,1:T(8,128)}, ...), condition=%wide.region_15.16_spmd.clone, body=%wide.region_13.15_spmd.clone.sunk | while | flops 1023474688 | bytes 107777264 | solution.py:259
  462.3 2.2 fusion.156
  466.2 3.7 fusion.158
  475.8 2.8 fusion.161
  478.6 2.9 fusion.162
  483.1 2.2 fusion.156
  487.0 3.7 fusion.158
  493.2 3.4 fusion.160
  496.7 3.4 fusion.161
  500.1 2.9 fusion.162
  504.6 2.2 fusion.156
  508.4 3.7 fusion.158
  514.7 3.4 fusion.160
  518.1 3.4 fusion.161
  521.5 2.9 fusion.162
  533.3 6.7 collective-permute-done.4
  541.6 7.8 collective-permute-done.5
  549.7 7.2 all_to_all.117
  560.0 7.2 all_to_all.118
  571.1 8.4 all_to_all.119
  587.0 6.6 convolution_convert_fusion.2
  593.7 6.6 convolution_convert_fusion.1
  601.2 6.7 convolution_convert_fusion
  609.4 12.3 reduce-scatter.10.cloned.1.call-done
  621.7 61.1 %reduce-scatter.12.cloned.1.call-done = bf16[64,512]{1,0:T(8,128)(2,1)} async-done(((bf16[1024,512]{1,0:T(8,128)(2,1)}), bf16[64,512]{1,0:T(8,128)(2,1)}) %reduce-scatter.12.cloned.1.call-update) | async-done | bytes 65552 | tf_op jit(solution)/shard_map/reduce_scatter | solution.py:309
  682.8 64.1 %reduce-scatter.14.cloned.1.call-done = bf16[64,1024]{1,0:T(8,128)(2,1)} async-done(((bf16[1024,1024]{1,0:T(8,128)(2,1)}), bf16[64,1024]{1,0:T(8,128)(2,1)}) %reduce-scatter.14.cloned.1.call-update) | async-done | bytes 131088 | tf_op jit(solution)/shard_map/reduce_scatter | solution.py:318
  746.9 64.8 %reduce-scatter.8.cloned.1.call-done = bf16[64,1024]{1,0:T(8,128)(2,1)} async-done(((bf16[1024,1024]{1,0:T(8,128)(2,1)}), bf16[64,1024]{1,0:T(8,128)(2,1)}) %reduce-scatter.8.cloned.1.call-update) | async-done | bytes 131088 | tf_op jit(solution)/shard_map/reduce_scatter | solution.py:303
  811.7 114.3 %reduce-scatter.16.cloned.1.call-done = bf16[64,4608]{1,0:T(8,128)(2,1)} async-done(((bf16[1024,4608]{1,0:T(8,128)(2,1)}), bf16[64,4608]{1,0:T(8,128)(2,1)}) %reduce-scatter.16.cloned.1.call-update) | async-done | bytes 589840 | tf_op jit(solution)/shard_map/reduce_scatter | solution.py:324
  926.1 115.8 %reduce-scatter.18.cloned.1.call-done = bf16[64,4608]{1,0:T(8,128)(2,1)} async-done(((bf16[1024,4608]{1,0:T(8,128)(2,1)}), bf16[64,4608]{1,0:T(8,128)(2,1)}) %reduce-scatter.18.cloned.1.call-update) | async-done | bytes 589840 | tf_op jit(solution)/shard_map/reduce_scatter | solution.py:327
  1041.9 115.1 %reduce-scatter.20.cloned.1.call-done = bf16[288,1024]{1,0:T(8,128)(2,1)} async-done(((bf16[4608,1024]{1,0:T(8,128)(2,1)}), bf16[288,1024]{1,0:T(8,128)(2,1)}) %reduce-scatter.20.cloned.1.call-update) | async-done | bytes 589840 | tf_op jit(solution)/shard_map/reduce_scatter | solution.py:330
  1157.0 7.1 fusion.48
  1166.9 32.4 %all-reduce.12 = (bf16[1024]{0:T(1024)(128)(2,1)S(1)}, bf16[64]{0:T(256)(128)(2,1)S(1)}, bf16[64]{0:T(256)(128)(2,1)S(1)}, bf16[1024]{0:T(1024)(128)(2,1)S(1)}) all-reduce(bf16[1024]{0:T(1024)(128)(2,1)S(1)} %get-tuple-element.276, bf16[64]{0:T(256)(128)(2,1)S(1)} %get-tuple-element.278, ...), channel_id=2, replica_groups=mesh['fsdp'=16,'seq'=2] {'fsdp'}, use_global_device_ids=true, to_apply=%region_20.21.clone | all-reduce | flops 2176 | bytes 8704
  1199.6 5.0 all-reduce.14
  1207.6 17.5 %all-reduce.18.cloned.1.call-done = (bf16[64,1024]{1,0:T(8,128)(2,1)}, bf16[64,512]{1,0:T(8,128)(2,1)}, bf16[64,512]{1,0:T(8,128)(2,1)}, bf16[64,1024]{1,0:T(8,1...) async-done(((bf16[64,1024]{1,0:T(8,128)(2,1)}, bf16[64,512]{1,0:T(8,128)(2,1)}, bf16[64,512]{1,0:T(8,128)(2,1)}, ...) | async-done | bytes 2162704 | tf_op jit(solution)/shard_map/psum | solution.py:336
  (318 shorter events, 110.2 us)
Async XLA Ops:
  7.2 83.0 %copy-start.6 = (bf16[192,1024]{1,0:T(8,128)(2,1)S(1)}, bf16[192,1024]{1,0:T(8,128)(2,1)}, u32[]{:S(2)}) copy-start(bf16[192,1024]{1,0:T(8,128)(2,1)} %param.18) | copy-start | bytes 1179652
  7.2 49.9 %all-gather.12.cloned.1.call-start = ((), (), s32[]{:S(2)}) async-start(), calls=%async_computation.17 | async-start | bytes 1114112 | tf_op jit(solution)/shard_map/all_gather | solution.py:122
  7.9 82.2 %all-gather.10.cloned.1.call-start = ((), (), s32[]{:S(2)}) async-start(), calls=%async_computation.16 | async-start | bytes 1114112 | tf_op jit(solution)/shard_map/all_gather | solution.py:121
  8.7 125.4 %all-gather.8.cloned.1.call-start = ((), (), s32[]{:S(2)}) async-start(), calls=%async_computation.15 | async-start | bytes 2228224 | tf_op jit(solution)/shard_map/all_gather | solution.py:120
  9.4 180.9 %all-gather.14.cloned.1.call-start = ((), (), s32[]{:S(2)}) async-start(), calls=%async_computation.18 | async-start | bytes 2228224 | tf_op jit(solution)/shard_map/all_gather | solution.py:125
  10.0 248.5 %all-gather.16.cloned.1.call-start = ((), (), s32[]{:S(2)}) async-start(), calls=%async_computation.19 | async-start | bytes 10027008 | tf_op jit(solution)/shard_map/all_gather | solution.py:127
  10.6 329.7 %all-gather.18.cloned.1.call-start = ((), (), s32[]{:S(2)}) async-start(), calls=%async_computation.20 | async-start | bytes 10027008 | tf_op jit(solution)/shard_map/all_gather | solution.py:128
  11.1 411.0 %all-gather.20.cloned.1.call-start = ((), (), s32[]{:S(2)}) async-start(), calls=%async_computation.21 | async-start | bytes 10027008 | tf_op jit(solution)/shard_map/all_gather | solution.py:129
  54.0 80.1 %copy-start.39 = (f32[1024]{0:T(1024)}, f32[1024]{0:T(1024)S(1)}, u32[]{:S(2)}) copy-start(f32[1024]{0:T(1024)S(1)} %convert_element_type.254) | copy-start | bytes 12292
  54.0 38.9 %copy-start.50 = (f32[64]{0:T(128)}, f32[64]{0:T(128)S(1)}, u32[]{:S(2)}) copy-start(f32[64]{0:T(128)S(1)} %convert_element_type.259) | copy-start | bytes 772
  56.8 77.3 %copy-start.46 = (f32[192]{0:T(256)}, f32[192]{0:T(256)S(1)}, u32[]{:S(2)}) copy-start(f32[192]{0:T(256)S(1)} %add_rsqrt_fusion.1) | copy-start | bytes 2308
  57.0 80.8 %copy-start.27 = (f32[192,32]{0,1:T(8,128)}, f32[192,32]{0,1:T(8,128)S(1)}, u32[]{:S(2)}) copy-start(f32[192,32]{0,1:T(8,128)S(1)} %get-tuple-element.380) | copy-start | bytes 73732
  57.1 80.8 %copy-start.29 = (f32[192,32]{0,1:T(8,128)}, f32[192,32]{0,1:T(8,128)S(1)}, u32[]{:S(2)}) copy-start(f32[192,32]{0,1:T(8,128)S(1)} %get-tuple-element.381) | copy-start | bytes 73732
  59.6 33.6 %all-to-all-start.2 = ((bf16[192,2,256]{2,0,1:T(8,128)(2,1)}), bf16[192,2,256]{2,0,1:T(8,128)(2,1)S(1)}, u32[]{:S(2)}, u32[]{:S(2)}) async-start(bf16[192,2,256]{2,0,1:T(8,128)(2,1)} %bitcast.212), calls=%async_computation.2 | async-start | bytes 393216 | tf_op jit(solution)/shard_map/all_to_all | solution.py:164
  100.8 2.6 collective-permute-start
  103.4 8.6 collective-permute-start.1
  110.5 26.2 %copy-start.52 = (f32[64]{0:T(128)}, f32[64]{0:T(128)S(1)}, u32[]{:S(2)}) copy-start(f32[64]{0:T(128)S(1)} %convert_element_type.256) | copy-start | bytes 772
  112.0 10.0 collective-permute-start.2
  139.1 11.0 all-to-all-start
  151.9 31.9 %copy-start.55 = (bf16[1024]{0:T(1024)(128)(2,1)S(1)}, bf16[1024]{0:T(1024)(128)(2,1)}, u32[]{:S(2)}) copy-start(bf16[1024]{0:T(1024)(128)(2,1)} %get-tuple-element.335) | copy-start | bytes 6148
  179.8 10.4 all-to-all-start.3
  190.3 75.7 %copy-start.18 = (bf16[2,24,8,512]{3,2,0,1:T(8,128)(2,1)}, bf16[2,24,8,512]{3,2,0,1:T(8,128)(2,1)S(1)}, u32[]{:S(2)}) copy-start(bf16[2,24,8,512]{3,2,0,1:T(8,128)(2,1)S(1)} %copy.158) | copy-start | bytes 1179652
  192.8 252.7 %copy-start.10 = (f32[192,1024]{1,0:T(8,128)}, f32[192,1024]{1,0:T(8,128)S(1)}, u32[]{:S(2)}) copy-start(f32[192,1024]{1,0:T(8,128)S(1)} %get-tuple-element.389) | copy-start | bytes 2359300
  192.9 147.3 %copy-start.8 = (bf16[192,1024]{1,0:T(8,128)(2,1)}, bf16[192,1024]{1,0:T(8,128)(2,1)S(1)}, u32[]{:S(2)}) copy-start(bf16[192,1024]{1,0:T(8,128)(2,1)S(1)} %multiply_convert_fusion.3) | copy-start | bytes 1179652
  433.4 8.2 copy-start.21
  433.4 8.2 copy-start.17
  433.4 8.2 copy-start.3
  441.6 3.9 copy-start.23
  447.1 14.5 %copy-start.12 = (f32[192,1024]{1,0:T(8,128)}, f32[192,1024]{1,0:T(8,128)S(1)}, u32[]{:S(2)}) copy-start(f32[192,1024]{1,0:T(8,128)S(1)} %multiply_add_fusion) | copy-start | bytes 2359300
  448.7 10.7 all-to-all-start.4
  452.2 169.5 %reduce-scatter.10.cloned.1.call-start = ((), (), s32[]{:S(2)}) async-start(), calls=%async_computation.23 | async-start | bytes 1114112 | tf_op jit(solution)/shard_map/reduce_scatter | solution.py:306
  469.8 2.6 copy-start
  472.4 3.4 copy-start.1
  493.2 3.4 copy-start.1
  514.7 3.4 copy-start.1
  526.1 4.8 copy-start.2
  528.3 3.6 collective-permute-start.3
  532.0 25.2 %copy-start.28 = (f32[192,32]{0,1:T(8,128)S(1)}, f32[192,32]{0,1:T(8,128)}, u32[]{:S(2)}) copy-start(f32[192,32]{0,1:T(8,128)} %copy-done.27) | copy-start | bytes 73732
  532.0 25.2 %copy-start.30 = (f32[192,32]{0,1:T(8,128)S(1)}, f32[192,32]{0,1:T(8,128)}, u32[]{:S(2)}) copy-start(f32[192,32]{0,1:T(8,128)} %copy-done.29) | copy-start | bytes 73732
  532.0 8.0 collective-permute-start.4
  540.1 17.1 %copy-start.16 = (f32[192,512]{0,1:T(8,128)S(1)}, f32[192,512]{0,1:T(8,128)}, u32[]{:S(2)}) copy-start(f32[192,512]{0,1:T(8,128)} %copy-done.15) | copy-start | bytes 1179652
  540.2 17.1 %copy-start.38 = (f32[192,8]{0,1:T(8,128)S(1)}, f32[192,8]{0,1:T(8,128)}, u32[]{:S(2)}) copy-start(f32[192,8]{0,1:T(8,128)} %copy-done.37) | copy-start | bytes 18436
  540.2 17.1 %copy-start.51 = (f32[64]{0:T(128)S(1)}, f32[64]{0:T(128)}, u32[]{:S(2)}) copy-start(f32[64]{0:T(128)} %copy-done.50) | copy-start | bytes 772
  540.2 9.2 collective-permute-start.5
  549.5 8.5 copy-start.45
  549.5 8.6 copy-start.7
  549.6 8.6 copy-start.40
  549.6 8.6 copy-start.47
  558.2 10.6 copy-start.13
  558.2 10.6 copy-start.19
  559.8 123.0 %reduce-scatter.12.cloned.1.call-start = ((), (), s32[]{:S(2)}) async-start(), calls=%async_computation.24 | async-start | bytes 1114112 | tf_op jit(solution)/shard_map/reduce_scatter | solution.py:309
  567.2 3.8 copy-start.31
  568.8 178.1 %reduce-scatter.14.cloned.1.call-start = ((), (), s32[]{:S(2)}) async-start(), calls=%async_computation.25 | async-start | bytes 2228224 | tf_op jit(solution)/shard_map/reduce_scatter | solution.py:318
  571.0 12.0 copy-start.5
  571.0 12.0 copy-start.36
  571.0 240.7 %reduce-scatter.8.cloned.1.call-start = ((), (), s32[]{:S(2)}) async-start(), calls=%async_computation.22 | async-start | bytes 2228224 | tf_op jit(solution)/shard_map/reduce_scatter | solution.py:303
  586.7 339.3 %reduce-scatter.16.cloned.1.call-start = ((), (), s32[]{:S(2)}) async-start(), calls=%async_computation.26 | async-start | bytes 10027008 | tf_op jit(solution)/shard_map/reduce_scatter | solution.py:324
  593.6 448.2 %reduce-scatter.18.cloned.1.call-start = ((), (), s32[]{:S(2)}) async-start(), calls=%async_computation.27 | async-start | bytes 10027008 | tf_op jit(solution)/shard_map/reduce_scatter | solution.py:327
  600.3 556.7 %reduce-scatter.20.cloned.1.call-start = ((), (), s32[]{:S(2)}) async-start(), calls=%async_computation.28 | async-start | bytes 10027008 | tf_op jit(solution)/shard_map/reduce_scatter | solution.py:330
  608.0 549.0 %copy-start.11 = (f32[192,1024]{1,0:T(8,128)S(1)}, f32[192,1024]{1,0:T(8,128)}, u32[]{:S(2)}) copy-start(f32[192,1024]{1,0:T(8,128)} %copy-done.10) | copy-start | bytes 2359300
  608.0 617.1 %all-reduce.18.cloned.1.call-start = ((), (), s32[]{:S(2)}) async-start(), calls=%async_computation.29 | async-start | bytes 4325376 | tf_op jit(solution)/shard_map/psum | solution.py:336
  1157.0 7.1 copy-start.20
  1225.1 8.5 copy-start.34
  1225.1 9.6 copy-start.33
  (21 other events, 37.0 us)
Sparse Core Ops, SparseCore 0:
  10.2 40.8 all-gather.11
  53.2 36.8 all-gather.9
  92.3 41.7 all-gather.7
  136.1 39.9 all-gather.13
  178.3 80.2 all-gather.15
  260.7 79.5 all-gather.17
  342.5 79.5 all-gather.19
  559.9 61.7 reduce-scatter.9
  626.3 56.4 reduce-scatter.11
  686.4 60.5 reduce-scatter.13
  751.1 60.5 reduce-scatter.7
  815.7 110.3 reduce-scatter.15
  930.7 111.1 reduce-scatter.17
  1045.8 111.1 reduce-scatter.19
  1159.8 65.2 all-reduce.17
where the time goes:
time: 1250 us; the launch traced here: 1240 us
  waiting for transfers between devices  858 us (69%)
  matrix products  145 us (12%)
  blocking collectives  104 us (8%)
  local copies, waits for them, and re-layouts  46.4 us (4%)
  starting transfers between devices  36.8 us (3%)
  other arithmetic  35.1 us (3%)
  between operations  18 us (1%)
    reduce_scatter x1, waiting for transfers between devices, on_device(): lax.psum_scatter(grad_up.astype(jnp.bfloat16), 'fsdp', scatter_dimension=...  116 us
    reduce_scatter x1, waiting for transfers between devices, on_device(): lax.psum_scatter(grad_down.astype(jnp.bfloat16), 'fsdp', scatter_dimensio...  115 us
    reduce_scatter x1, waiting for transfers between devices, on_device(): lax.psum_scatter(grad_gate.astype(jnp.bfloat16), 'fsdp', scatter_dimensio...  114 us
    all_gather x1, waiting for transfers between devices, on_device(): lax.all_gather(down_weight, 'fsdp', axis=0, tiled=True)  74.4 us
    all_gather x1, waiting for transfers between devices, on_device(): lax.all_gather(up_weight, 'fsdp', axis=0, tiled=True)  74.3 us
    unnamed x2, blocking collectives  68.5 us
    all_gather x1, waiting for transfers between devices, on_device(): lax.all_gather(gate_weight, 'fsdp', axis=0, tiled=True)  65.6 us
    reduce_scatter x1, waiting for transfers between devices, on_device(): lax.psum_scatter(grad_query.astype(jnp.bfloat16), 'fsdp', scatter_dimensi...  64.8 us
  transfers between devices with their start and end apart: 25, of which 20 were waited for; matrix products, arithmetic and copies ran while one was open for 9% of the time, Pallas kernels for 0%

commit v1 on v0

--- a/solution.py
+++ b/solution.py
@@ -115,6 +115,39 @@
         ]
     )
     key_start = doc_start(starts, key_place)
+
+    def start_the_space(sheet):
+        s_next, carry_in, piece_out = (
+            lax.axis_size("fsdp"),
+            lax.axis_index("fsdp"),
+            sheet.shape[0],
+        )
+        after = y_new = sheet
+        raw_out = lax.dynamic_update_slice_in_dim(
+            jnp.zeros(
+                [j * s_next if dev_i == 0 else j for dev_i, j in enumerate(sheet.shape)],
+                sheet.dtype,
+            ),
+            sheet,
+            carry_in * piece_out,
+            axis=0,
+        )
+        for at in range(1, s_next // 2 + 1):
+            after = lax.ppermute(
+                after, "fsdp", perm=[(dev_i, (dev_i + 1) % s_next) for dev_i in range(s_next)]
+            )
+            raw_out = lax.dynamic_update_slice_in_dim(
+                raw_out, after, (carry_in - at) % s_next * piece_out, axis=0
+            )
+            if 2 * at < s_next:
+                y_new = lax.ppermute(
+                    y_new, "fsdp", [(dev_i, (dev_i - 1) % s_next) for dev_i in range(s_next)]
+                )
+                raw_out = lax.dynamic_update_slice_in_dim(
+                    raw_out, y_new, (carry_in + at) % s_next * piece_out, axis=0
+                )
+        return raw_out
+
     gathered = (
         lax.all_gather(attention_gain, "fsdp", axis=0, tiled=True),
         lax.all_gather(query_weight, "fsdp", axis=0, tiled=True),
@@ -126,7 +159,7 @@
         lax.all_gather(feedforward_gain, "fsdp", axis=0, tiled=True),
         lax.all_gather(gate_weight, "fsdp", axis=0, tiled=True),
         lax.all_gather(up_weight, "fsdp", axis=0, tiled=True),
-        lax.all_gather(down_weight, "fsdp", axis=0, tiled=True),
+        start_the_space(down_weight),
     )
     gain_one = gathered[0].astype(jnp.float32)
     full_query = gathered[1]

time: 1250 us -> 1210 us (0.968)
  waiting for transfers between devices: 858 us -> 749 us
  starting transfers between devices: 36.8 us -> 85.7 us
  local copies, waits for them, and re-layouts: 46.4 us -> 74.9 us
    all_gather x1 -> x0, waiting for transfers between devices: 74.4 us -> none  [on_device(): lax.all_gather(down_weight, 'fsdp', axis=0, tiled=True)]
    ppermute x0 -> x15, starting transfers between devices: none -> 38.9 us  [the longest x8 20.3 us: start_the_space(): lax.ppermute(after, 'fsdp', perm=[(dev_i, (dev_i + 1) % s_next) for dev_i...]
    all_gather x1, waiting for transfers between devices: 27.1 us -> 0.01 us  [on_device(): lax.all_gather(key_matrix, 'fsdp', axis=0, tiled=True)]
    dynamic_update_slice x0 -> x16, local copies, waits for them, and re-layouts: none -> 26.9 us  [the longest x8 13.5 us: start_the_space(): lax.dynamic_update_slice_in_dim(raw_out, after, (carry_in - at) % s_next...]
  transfers between devices with their start and end apart: 25 -> 40, of which waited for: 20 -> 18; matrix products, arithmetic and copies ran while one was open for 9% -> 11% of each run, Pallas kernels for 0% -> 0%
where the time goes in v1:
time: 1210 us; the launch traced here: 1200 us
  waiting for transfers between devices  749 us (62%)
  matrix products  135 us (11%)
  blocking collectives  99.7 us (8%)
  starting transfers between devices  85.7 us (7%)
  local copies, waits for them, and re-layouts  74.9 us (6%)
  other arithmetic  32.1 us (3%)
  between operations  18 us (1%)
    reduce_scatter x1, waiting for transfers between devices, on_device(): lax.psum_scatter(grad_up.astype(jnp.bfloat16), 'fsdp', scatter_dimension=...  116 us
    reduce_scatter x1, waiting for transfers between devices, on_device(): lax.psum_scatter(grad_down.astype(jnp.bfloat16), 'fsdp', scatter_dimensio...  115 us
    reduce_scatter x1, waiting for transfers between devices, on_device(): lax.psum_scatter(grad_gate.astype(jnp.bfloat16), 'fsdp', scatter_dimensio...  114 us
    all_gather x1, waiting for transfers between devices, on_device(): lax.all_gather(up_weight, 'fsdp', axis=0, tiled=True)  74.2 us
    unnamed x2, blocking collectives  71.9 us
    reduce_scatter x1, waiting for transfers between devices, on_device(): lax.psum_scatter(grad_query.astype(jnp.bfloat16), 'fsdp', scatter_dimensi...  64.7 us
    all_gather x1, waiting for transfers between devices, on_device(): lax.all_gather(gate_weight, 'fsdp', axis=0, tiled=True)  64.5 us
    reduce_scatter x1, waiting for transfers between devices, on_device(): lax.psum_scatter(grad_output.astype(jnp.bfloat16), 'fsdp', scatter_dimens...  64.3 us
  transfers between devices with their start and end apart: 40, of which 18 were waited for; matrix products, arithmetic and copies ran while one was open for 11% of the time, Pallas kernels for 0%

profile of v1, /device:TPU:0, one launch (start us, length us, event | category | flops | bytes accessed | tf_op | source)
XLA Modules:
  0.0 1195.4 jit_solution(14154277808477352932)
XLA Ops:
  11.1 5.1 collective-permute-start.4
  19.3 4.8 broadcast_in_dim.62
  25.2 2.7 collective-permute-start.5
  32.6 39.3 %all-reduce.13 = (bf16[64]{0:T(256)(128)(2,1)S(1)}, bf16[1024]{0:T(1024)(128)(2,1)S(1)}, bf16[64]{0:T(256)(128)(2,1)S(1)}, bf16[1024]{0:T(1024)(128)(2,1)S(1)}) all-reduce(bf16[64]{0:T(256)(128)(2,1)S(1)} %dynamic-update-slice.1, bf16[1024]{0:T(1024)(128)(2,1)S(1)} %dynamic-update-slice, ...), channel_id=1, replica_groups=mesh['fsdp'=16,'seq'=2] {'fsdp'}, use_global_device_ids=true, to_apply=%add.5 | all-reduce | flops 2176 | bytes 8704
  73.6 4.4 collective-permute-start.8
  81.7 3.4 all-to-all-start.1
  85.1 12.3 %all-gather.11.cloned.1.call-done = bf16[1024,512]{1,0:T(8,128)(2,1)} async-done(((bf16[64,512]{1,0:T(8,128)(2,1)}), bf16[1024,512]{1,0:T(8,128)(2,1)}) %all-gather.11.cloned.1.call-update) | async-done | bytes 1048592 | tf_op jit(solution)/shard_map/all_gather | solution.py:155
  99.8 3.4 all-to-all-start.2
  104.3 4.2 collective-permute-start.10
  118.5 3.2 collective-permute-start.11
  123.0 11.1 collective-permute-start.1
  138.4 11.9 collective-permute-start.2
  150.6 2.5 collective-permute-start.13
  163.1 8.4 collective-permute-start.15
  171.6 2.6 multiply_reduce_fusion.2
  176.6 3.5 all-to-all-start
  184.0 2.6 collective-permute-start.17
  188.4 21.2 %while.27 = (s32[]{:T(128)}, bf16[3,128,512]{2,1,0:T(8,128)(2,1)}, f32[3,4,2,128]{3,2,1,0:T(2,128)}, s32[1536]{0:T(1024)S(1)}, s32[3,128]{1,0:T(4,128)}, /*index...) while((s32[]{:T(128)}, bf16[3,128,512]{2,1,0:T(8,128)(2,1)}, ...), condition=%wide.region_10.11_spmd, body=%wide.region_7.10_spmd.sunk | while | flops 422181888 | bytes 22069364 | solution.py:244
  209.6 3.5 all-to-all-start.3
  216.9 3.0 all-to-all-done.3
  220.0 2.4 multiply_reduce_fusion.5
  226.0 64.5 %all-gather.15.cloned.1.call-done = bf16[1024,4608]{1,0:T(8,128)(2,1)} async-done(((bf16[64,4608]{1,0:T(8,128)(2,1)}), bf16[1024,4608]{1,0:T(8,128)(2,1)}) %all-gather.15.cloned.1.call-update) | async-done | bytes 9437200 | tf_op jit(solution)/shard_map/all_gather | solution.py:160
  290.5 7.5 fusion.85
  298.1 74.2 %all-gather.17.cloned.1.call-done = bf16[1024,4608]{1,0:T(8,128)(2,1)} async-done(((bf16[64,4608]{1,0:T(8,128)(2,1)}), bf16[1024,4608]{1,0:T(8,128)(2,1)}) %all-gather.17.cloned.1.call-update) | async-done | bytes 9437200 | tf_op jit(solution)/shard_map/all_gather | solution.py:161
  372.3 7.6 fusion.86
  380.0 12.8 %multiply_convert_fusion = (bf16[192,4608]{1,0:T(8,128)(2,1)}, bf16[192,4608]{1,0:T(8,128)(2,1)}, bf16[192,4608]{1,0:T(8,128)(2,1)}) fusion(f32[192,4608]{1,0:T(8,128)S(1)} %copy-done.23, f32[192,4608]{1,0:T(8,128)} %fusion.86, bf16[4608,1024]{1,0:T(8,128)(2,1)} %constant_dynamic-update-slice_fusion.2, bf16[192,1024]{1,0:T(8,128)(2,1)S(1)} %copy-done.28), kind=kOutput, calls=%fused_computation.67 | convolution fusion | flops 1826095104 | bytes 22216704 | tf_op jit(solution)/shard_map/dot_general | solution.py:33
  392.9 4.7 fusion.87
  397.6 5.4 multiply_reduce_fusion.3
  405.8 3.5 all-to-all-start.4
  409.7 6.8 all-to-all-done.4
  418.3 62.3 %while.28 = (s32[]{:T(128)}, f32[1536,4,64]{0,2,1:T(8,128)}, f32[1536,4,64]{0,2,1:T(8,128)}, bf16[3,128,512]{2,1,0:T(8,128)(2,1)}, bf16[3,128,4,2,64]{1,4,3,2,0:...) while((s32[]{:T(128)}, f32[1536,4,64]{0,2,1:T(8,128)}, ...), condition=%wide.region_15.16_spmd.clone, body=%wide.region_13.15_spmd.clone.sunk | while | flops 1023474688 | bytes 98341240 | solution.py:292
  421.0 2.4 fusion.158
  423.4 2.6 copy-done
  428.5 2.9 fusion.162
  433.0 4.8 fusion.161
  440.5 2.4 fusion.158
  443.0 2.6 copy-done
  446.2 3.2 fusion.160
  449.4 2.9 fusion.162
  454.0 5.2 fusion.161
  461.9 2.4 fusion.158
  464.4 2.6 copy-done
  467.6 3.2 fusion.160
  470.8 2.9 fusion.162
  475.3 5.2 fusion.161
  488.0 6.8 collective-permute-done.19
  496.1 7.8 collective-permute-done.20
  504.2 7.2 all_to_all.116
  514.6 7.2 all_to_all.117
  525.7 8.4 all_to_all.118
  540.1 6.7 convolution_convert_fusion.2
  546.9 6.5 convolution_convert_fusion.1
  554.4 6.6 convolution_convert_fusion
  562.4 14.0 %reduce-scatter.10.cloned.1.call-done = bf16[64,512]{1,0:T(8,128)(2,1)} async-done(((bf16[1024,512]{1,0:T(8,128)(2,1)}), bf16[64,512]{1,0:T(8,128)(2,1)}) %reduce-scatter.10.cloned.1.call-update) | async-done | bytes 65552 | tf_op jit(solution)/shard_map/reduce_scatter | solution.py:339
  576.4 60.5 %reduce-scatter.12.cloned.1.call-done = bf16[64,512]{1,0:T(8,128)(2,1)} async-done(((bf16[1024,512]{1,0:T(8,128)(2,1)}), bf16[64,512]{1,0:T(8,128)(2,1)}) %reduce-scatter.12.cloned.1.call-update) | async-done | bytes 65552 | tf_op jit(solution)/shard_map/reduce_scatter | solution.py:342
  636.9 64.3 %reduce-scatter.14.cloned.1.call-done = bf16[64,1024]{1,0:T(8,128)(2,1)} async-done(((bf16[1024,1024]{1,0:T(8,128)(2,1)}), bf16[64,1024]{1,0:T(8,128)(2,1)}) %reduce-scatter.14.cloned.1.call-update) | async-done | bytes 131088 | tf_op jit(solution)/shard_map/reduce_scatter | solution.py:351
  701.2 64.7 %reduce-scatter.8.cloned.1.call-done = bf16[64,1024]{1,0:T(8,128)(2,1)} async-done(((bf16[1024,1024]{1,0:T(8,128)(2,1)}), bf16[64,1024]{1,0:T(8,128)(2,1)}) %reduce-scatter.8.cloned.1.call-update) | async-done | bytes 131088 | tf_op jit(solution)/shard_map/reduce_scatter | solution.py:336
  765.9 114.5 %reduce-scatter.16.cloned.1.call-done = bf16[64,4608]{1,0:T(8,128)(2,1)} async-done(((bf16[1024,4608]{1,0:T(8,128)(2,1)}), bf16[64,4608]{1,0:T(8,128)(2,1)}) %reduce-scatter.16.cloned.1.call-update) | async-done | bytes 589840 | tf_op jit(solution)/shard_map/reduce_scatter | solution.py:357
  880.4 115.7 %reduce-scatter.18.cloned.1.call-done = bf16[64,4608]{1,0:T(8,128)(2,1)} async-done(((bf16[1024,4608]{1,0:T(8,128)(2,1)}), bf16[64,4608]{1,0:T(8,128)(2,1)}) %reduce-scatter.18.cloned.1.call-update) | async-done | bytes 589840 | tf_op jit(solution)/shard_map/reduce_scatter | solution.py:360
  996.0 115.2 %reduce-scatter.20.cloned.1.call-done = bf16[288,1024]{1,0:T(8,128)(2,1)} async-done(((bf16[4608,1024]{1,0:T(8,128)(2,1)}), bf16[288,1024]{1,0:T(8,128)(2,1)}) %reduce-scatter.20.cloned.1.call-update) | async-done | bytes 589840 | tf_op jit(solution)/shard_map/reduce_scatter | solution.py:363
  1111.3 7.1 fusion.48
  1120.7 32.6 %all-reduce.12 = (bf16[1024]{0:T(1024)(128)(2,1)S(1)}, bf16[64]{0:T(256)(128)(2,1)S(1)}, bf16[64]{0:T(256)(128)(2,1)S(1)}, bf16[1024]{0:T(1024)(128)(2,1)S(1)}) all-reduce(bf16[1024]{0:T(1024)(128)(2,1)S(1)} %get-tuple-element.276, bf16[64]{0:T(256)(128)(2,1)S(1)} %get-tuple-element.278, ...), channel_id=2, replica_groups=mesh['fsdp'=16,'seq'=2] {'fsdp'}, use_global_device_ids=true, to_apply=%region_20.21.clone | all-reduce | flops 2176 | bytes 8704
  1153.6 5.0 all-reduce.14
  1161.6 17.8 %all-reduce.18.cloned.1.call-done = (bf16[64,1024]{1,0:T(8,128)(2,1)}, bf16[64,512]{1,0:T(8,128)(2,1)}, bf16[64,512]{1,0:T(8,128)(2,1)}, bf16[64,1024]{1,0:T(8,1...) async-done(((bf16[64,1024]{1,0:T(8,128)(2,1)}, bf16[64,512]{1,0:T(8,128)(2,1)}, bf16[64,512]{1,0:T(8,128)(2,1)}, ...) | async-done | bytes 2162704 | tf_op jit(solution)/shard_map/psum | solution.py:369
  (421 shorter events, 141.8 us)
Async XLA Ops:
  7.2 70.9 %all-gather.9.cloned.1.call-start = ((), (), s32[]{:S(2)}) async-start(), calls=%async_computation.16 | async-start | bytes 1114112 | tf_op jit(solution)/shard_map/all_gather | solution.py:154
  7.9 89.5 %all-gather.11.cloned.1.call-start = ((), (), s32[]{:S(2)}) async-start(), calls=%async_computation.17 | async-start | bytes 1114112 | tf_op jit(solution)/shard_map/all_gather | solution.py:155
  8.7 162.9 %all-gather.7.cloned.1.call-start = ((), (), s32[]{:S(2)}) async-start(), calls=%async_computation.15 | async-start | bytes 2228224 | tf_op jit(solution)/shard_map/all_gather | solution.py:153
  9.4 210.6 %all-gather.13.cloned.1.call-start = ((), (), s32[]{:S(2)}) async-start(), calls=%async_computation.18 | async-start | bytes 2228224 | tf_op jit(solution)/shard_map/all_gather | solution.py:158
  10.0 280.6 %all-gather.15.cloned.1.call-start = ((), (), s32[]{:S(2)}) async-start(), calls=%async_computation.19 | async-start | bytes 10027008 | tf_op jit(solution)/shard_map/all_gather | solution.py:160
  10.6 361.7 %all-gather.17.cloned.1.call-start = ((), (), s32[]{:S(2)}) async-start(), calls=%async_computation.20 | async-start | bytes 10027008 | tf_op jit(solution)/shard_map/all_gather | solution.py:161
  10.6 14.6 %collective-permute-start.3 = (bf16[288,1024]{1,0:T(8,128)(2,1)}, bf16[288,1024]{1,0:T(8,128)(2,1)S(1)}, u32[]{:S(2)}, u32[]{:S(2)}) collective-permute-start(bf16[288,1024]{1,0:T(8,128)(2,1)} %param.31), channel_id=1, source_target_pairs={{0,2},{2,4},{4,6},{6,8},{8,10},{10,12},{12,14},{14,16},{16,18},{18... | collective-permute-start | bytes 1769480 | tf_op jit(solution)/shard_map/ppermute | solution.py:136
  11.1 16.8 %collective-permute-start.4 = (bf16[288,1024]{1,0:T(8,128)(2,1)}, bf16[288,1024]{1,0:T(8,128)(2,1)S(1)}, u32[]{:S(2)}, u32[]{:S(2)}) collective-permute-start(bf16[288,1024]{1,0:T(8,128)(2,1)} %param.31), channel_id=1, source_target_pairs={{0,30},{2,0},{4,2},{6,4},{8,6},{10,8},{12,10},{14,12},{16,14},{18,... | collective-permute-start | bytes 1769480 | tf_op jit(solution)/shard_map/ppermute | solution.py:143
  19.3 13.1 %copy-start.67 = (bf16[4]{0:T(256)(128)(2,1)S(1)}, bf16[4]{0:T(256)(128)(2,1)}, u32[]{:S(2)}) copy-start(bf16[4]{0:T(256)(128)(2,1)} %param.26) | copy-start | bytes 28
  25.2 146.4 %copy-start.54 = (f32[192]{0:T(256)}, f32[192]{0:T(256)S(1)}, u32[]{:S(2)}) copy-start(f32[192]{0:T(256)S(1)} %add_rsqrt_fusion.1) | copy-start | bytes 2308
  25.2 48.4 %collective-permute-start.5 = (bf16[288,1024]{1,0:T(8,128)(2,1)S(1)}, bf16[288,1024]{1,0:T(8,128)(2,1)S(1)}, u32[]{:S(2)}, u32[]{:S(2)}) collective-permute-start(bf16[288,1024]{1,0:T(8,128)(2,1)S(1)} %collective-permute-done.3), channel_id=1, source_target_pairs={{0,2},{2,4},{4,6},{6,8},{8,10},{10,12},{12,14},{14,16},{16,18},{18... | collective-permute-start | bytes 1769480 | tf_op jit(solution)/shard_map/ppermute | solution.py:136
  27.9 45.7 %collective-permute-start.6 = (bf16[288,1024]{1,0:T(8,128)(2,1)S(1)}, bf16[288,1024]{1,0:T(8,128)(2,1)}, u32[]{:S(2)}, u32[]{:S(2)}) collective-permute-start(bf16[288,1024]{1,0:T(8,128)(2,1)S(1)} %collective-permute-done.4), channel_id=1, source_target_pairs={{0,30},{2,0},{4,2},{6,4},{8,6},{10,8},{12,10},{14,12},{16,14},{18,... | collective-permute-start | bytes 1769480 | tf_op jit(solution)/shard_map/ppermute | solution.py:143
  71.9 99.7 %copy-start.45 = (f32[1024]{0:T(1024)}, f32[1024]{0:T(1024)S(1)}, u32[]{:S(2)}) copy-start(f32[1024]{0:T(1024)S(1)} %convert_element_type.254) | copy-start | bytes 12292
  71.9 27.2 %copy-start.59 = (f32[64]{0:T(128)}, f32[64]{0:T(128)S(1)}, u32[]{:S(2)}) copy-start(f32[64]{0:T(128)S(1)} %convert_element_type.259) | copy-start | bytes 772
  71.9 102.3 %copy-start.61 = (f32[64]{0:T(128)}, f32[64]{0:T(128)S(1)}, u32[]{:S(2)}) copy-start(f32[64]{0:T(128)S(1)} %convert_element_type.256) | copy-start | bytes 772
  72.7 102.7 %copy-start.32 = (f32[192,32]{0,1:T(8,128)}, f32[192,32]{0,1:T(8,128)S(1)}, u32[]{:S(2)}) copy-start(f32[192,32]{0,1:T(8,128)S(1)} %get-tuple-element.380) | copy-start | bytes 73732
  72.7 102.7 %copy-start.34 = (f32[192,32]{0,1:T(8,128)}, f32[192,32]{0,1:T(8,128)S(1)}, u32[]{:S(2)}) copy-start(f32[192,32]{0,1:T(8,128)S(1)} %get-tuple-element.381) | copy-start | bytes 73732
  73.6 30.5 %collective-permute-start.7 = (bf16[288,1024]{1,0:T(8,128)(2,1)S(1)}, bf16[288,1024]{1,0:T(8,128)(2,1)}, u32[]{:S(2)}, u32[]{:S(2)}) collective-permute-start(bf16[288,1024]{1,0:T(8,128)(2,1)S(1)} %collective-permute-done.5), channel_id=1, source_target_pairs={{0,2},{2,4},{4,6},{6,8},{8,10},{10,12},{12,14},{14,16},{16,18},{18... | collective-permute-start | bytes 1769480 | tf_op jit(solution)/shard_map/ppermute | solution.py:136
  73.6 30.7 %collective-permute-start.8 = (bf16[288,1024]{1,0:T(8,128)(2,1)}, bf16[288,1024]{1,0:T(8,128)(2,1)}, u32[]{:S(2)}, u32[]{:S(2)}) collective-permute-start(bf16[288,1024]{1,0:T(8,128)(2,1)} %collective-permute-done.6), channel_id=1, source_target_pairs={{0,30},{2,0},{4,2},{6,4},{8,6},{10,8},{12,10},{14,12},{16,14},{18,... | collective-permute-start | bytes 1769480 | tf_op jit(solution)/shard_map/ppermute | solution.py:143
  79.9 30.9 %copy-start.52 = (f32[192,8]{0,1:T(8,128)}, f32[192,8]{0,1:T(8,128)S(1)}, u32[]{:S(2)}) copy-start(f32[192,8]{0,1:T(8,128)S(1)} %get-tuple-element.386) | copy-start | bytes 18436
  79.9 28.6 %copy-start.41 = (f32[192,8]{0,1:T(8,128)}, f32[192,8]{0,1:T(8,128)S(1)}, u32[]{:S(2)}) copy-start(f32[192,8]{0,1:T(8,128)S(1)} %fusion.69) | copy-start | bytes 18436
  81.7 18.1 %all-to-all-start.1 = ((bf16[192,2,256]{2,0,1:T(8,128)(2,1)}), bf16[192,2,256]{2,0,1:T(8,128)(2,1)S(1)}, u32[]{:S(2)}, u32[]{:S(2)}) async-start(bf16[192,2,256]{2,0,1:T(8,128)(2,1)} %copy.117), calls=%async_computation.1 | async-start | bytes 393216 | tf_op jit(solution)/shard_map/all_to_all | solution.py:194
  99.8 8.8 all-to-all-start.2
  104.1 14.5 %collective-permute-start.9 = (bf16[288,1024]{1,0:T(8,128)(2,1)}, bf16[288,1024]{1,0:T(8,128)(2,1)}, u32[]{:S(2)}, u32[]{:S(2)}) collective-permute-start(bf16[288,1024]{1,0:T(8,128)(2,1)} %collective-permute-done.7), channel_id=1, source_target_pairs={{0,2},{2,4},{4,6},{6,8},{8,10},{10,12},{12,14},{14,16},{16,18},{18... | collective-permute-start | bytes 1769480 | tf_op jit(solution)/shard_map/ppermute | solution.py:136
  104.3 17.4 %collective-permute-start.10 = (bf16[288,1024]{1,0:T(8,128)(2,1)}, bf16[288,1024]{1,0:T(8,128)(2,1)}, u32[]{:S(2)}, u32[]{:S(2)}) collective-permute-start(bf16[288,1024]{1,0:T(8,128)(2,1)} %collective-permute-done.8), channel_id=1, source_target_pairs={{0,30},{2,0},{4,2},{6,4},{8,6},{10,8},{12,10},{14,12},{16,14},{18,... | collective-permute-start | bytes 1769480 | tf_op jit(solution)/shard_map/ppermute | solution.py:143
  108.6 14.4 %collective-permute-start = (bf16[2,384,256]{2,1,0:T(8,128)(2,1)S(1)}, bf16[2,384,256]{2,1,0:T(8,128)(2,1)S(1)}, u32[]{:S(2)}, u32[]{:S(2)}) collective-permute-start(bf16[2,384,256]{2,1,0:T(8,128)(2,1)S(1)} %pad_maximum_fusion.3), channel_id=1, source_target_pairs={{0,2},{2,4},{4,6},{6,8},{8,10},{10,12},{12,14},{14,16},{16,18},{18... | collective-permute-start | bytes 1179656 | tf_op jit(solution)/shard_map/ppermute | solution.py:19
  118.5 32.1 %collective-permute-start.11 = (bf16[288,1024]{1,0:T(8,128)(2,1)}, bf16[288,1024]{1,0:T(8,128)(2,1)}, u32[]{:S(2)}, u32[]{:S(2)}) collective-permute-start(bf16[288,1024]{1,0:T(8,128)(2,1)} %collective-permute-done.9), channel_id=1, source_target_pairs={{0,2},{2,4},{4,6},{6,8},{8,10},{10,12},{12,14},{14,16},{16,18},{18... | collective-permute-start | bytes 1769480 | tf_op jit(solution)/shard_map/ppermute | solution.py:136
  121.8 31.4 %collective-permute-start.12 = (bf16[288,1024]{1,0:T(8,128)(2,1)}, bf16[288,1024]{1,0:T(8,128)(2,1)}, u32[]{:S(2)}, u32[]{:S(2)}) collective-permute-start(bf16[288,1024]{1,0:T(8,128)(2,1)} %collective-permute-done.10), channel_id=1, source_target_pairs={{0,30},{2,0},{4,2},{6,4},{8,6},{10,8},{12,10},{14,12},{16,14},{18,... | collective-permute-start | bytes 1769480 | tf_op jit(solution)/shard_map/ppermute | solution.py:143
  123.0 15.4 %collective-permute-start.1 = (bf16[2,384,256]{2,1,0:T(8,128)(2,1)S(1)}, bf16[2,384,256]{2,1,0:T(8,128)(2,1)S(1)}, u32[]{:S(2)}, u32[]{:S(2)}) collective-permute-start(bf16[2,384,256]{2,1,0:T(8,128)(2,1)S(1)} %collective-permute-done), channel_id=1, source_target_pairs={{0,2},{2,4},{4,6},{6,8},{8,10},{10,12},{12,14},{14,16},{16,18},{18... | collective-permute-start | bytes 1179656 | tf_op jit(solution)/shard_map/ppermute | solution.py:19
  138.4 20.7 %collective-permute-start.2 = (bf16[2,384,256]{2,1,0:T(8,128)(2,1)S(1)}, bf16[2,384,256]{2,1,0:T(8,128)(2,1)S(1)}, u32[]{:S(2)}, u32[]{:S(2)}) collective-permute-start(bf16[2,384,256]{2,1,0:T(8,128)(2,1)S(1)} %collective-permute-done.1), channel_id=1, source_target_pairs={{0,2},{2,4},{4,6},{6,8},{8,10},{10,12},{12,14},{14,16},{16,18},{18... | collective-permute-start | bytes 1179656 | tf_op jit(solution)/shard_map/ppermute | solution.py:19
  150.6 12.5 %collective-permute-start.13 = (bf16[288,1024]{1,0:T(8,128)(2,1)}, bf16[288,1024]{1,0:T(8,128)(2,1)}, u32[]{:S(2)}, u32[]{:S(2)}) collective-permute-start(bf16[288,1024]{1,0:T(8,128)(2,1)} %collective-permute-done.11), channel_id=1, source_target_pairs={{0,2},{2,4},{4,6},{6,8},{8,10},{10,12},{12,14},{14,16},{16,18},{18... | collective-permute-start | bytes 1769480 | tf_op jit(solution)/shard_map/ppermute | solution.py:136
  153.2 18.4 %collective-permute-start.14 = (bf16[288,1024]{1,0:T(8,128)(2,1)}, bf16[288,1024]{1,0:T(8,128)(2,1)}, u32[]{:S(2)}, u32[]{:S(2)}) collective-permute-start(bf16[288,1024]{1,0:T(8,128)(2,1)} %collective-permute-done.12), channel_id=1, source_target_pairs={{0,30},{2,0},{4,2},{6,4},{8,6},{10,8},{12,10},{14,12},{16,14},{18,... | collective-permute-start | bytes 1769480 | tf_op jit(solution)/shard_map/ppermute | solution.py:143
  163.1 20.9 %collective-permute-start.15 = (bf16[288,1024]{1,0:T(8,128)(2,1)}, bf16[288,1024]{1,0:T(8,128)(2,1)}, u32[]{:S(2)}, u32[]{:S(2)}) collective-permute-start(bf16[288,1024]{1,0:T(8,128)(2,1)} %collective-permute-done.13), channel_id=1, source_target_pairs={{0,2},{2,4},{4,6},{6,8},{8,10},{10,12},{12,14},{14,16},{16,18},{18... | collective-permute-start | bytes 1769480 | tf_op jit(solution)/shard_map/ppermute | solution.py:136
  171.6 43.4 %collective-permute-start.16 = (bf16[288,1024]{1,0:T(8,128)(2,1)}, bf16[288,1024]{1,0:T(8,128)(2,1)}, u32[]{:S(2)}, u32[]{:S(2)}) collective-permute-start(bf16[288,1024]{1,0:T(8,128)(2,1)} %collective-permute-done.14), channel_id=1, source_target_pairs={{0,30},{2,0},{4,2},{6,4},{8,6},{10,8},{12,10},{14,12},{16,14},{18,... | collective-permute-start | bytes 1769480 | tf_op jit(solution)/shard_map/ppermute | solution.py:143
  176.6 10.0 all-to-all-start
  184.0 39.9 %collective-permute-start.17 = (bf16[288,1024]{1,0:T(8,128)(2,1)}, bf16[288,1024]{1,0:T(8,128)(2,1)}, u32[]{:S(2)}, u32[]{:S(2)}) collective-permute-start(bf16[288,1024]{1,0:T(8,128)(2,1)} %collective-permute-done.15), channel_id=1, source_target_pairs={{0,2},{2,4},{4,6},{6,8},{8,10},{10,12},{12,14},{14,16},{16,18},{18... | collective-permute-start | bytes 1769480 | tf_op jit(solution)/shard_map/ppermute | solution.py:136
  209.6 10.4 all-to-all-start.3
  220.0 78.1 %copy-start.21 = (bf16[2,24,8,512]{3,2,0,1:T(8,128)(2,1)}, bf16[2,24,8,512]{3,2,0,1:T(8,128)(2,1)S(1)}, u32[]{:S(2)}) copy-start(bf16[2,24,8,512]{3,2,0,1:T(8,128)(2,1)S(1)} %copy.158) | copy-start | bytes 1179652
  222.4 180.6 %copy-start.12 = (f32[192,1024]{1,0:T(8,128)}, f32[192,1024]{1,0:T(8,128)S(1)}, u32[]{:S(2)}) copy-start(f32[192,1024]{1,0:T(8,128)S(1)} %get-tuple-element.389) | copy-start | bytes 2359300
  223.9 148.4 %copy-start.10 = (bf16[192,1024]{1,0:T(8,128)(2,1)}, bf16[192,1024]{1,0:T(8,128)(2,1)S(1)}, u32[]{:S(2)}) copy-start(bf16[192,1024]{1,0:T(8,128)(2,1)S(1)} %multiply_convert_fusion.3) | copy-start | bytes 1179652
  372.3 20.5 %slice-start.3 = ((s8[9437184]{0:T(1024)(128)(4,1)}), s8[4194304]{0:T(1024)(128)(4,1)S(1)}, s32[]{:S(2)}) async-start(s8[9437184]{0:T(1024)(128)(4,1)} %bitcast.270), calls=%async_computation.32 | async-start | bytes 8388608
  372.3 25.2 %slice-start = ((s8[9437184]{0:T(1024)(128)(4,1)}), s8[4194304]{0:T(1024)(128)(4,1)S(1)}, s32[]{:S(2)}) async-start(s8[9437184]{0:T(1024)(128)(4,1)} %bitcast.267), calls=%async_computation.29 | async-start | bytes 8388608
  379.9 12.9 %slice-start.5 = ((s8[9437184]{0:T(1024)(128)(4,1)}), s8[1048576]{0:T(1024)(128)(4,1)S(1)}, s32[]{:S(2)}) async-start(s8[9437184]{0:T(1024)(128)(4,1)} %bitcast.270), calls=%async_computation.34 | async-start | bytes 2097152
  379.9 17.6 %slice-start.1 = ((s8[9437184]{0:T(1024)(128)(4,1)}), s8[4194304]{0:T(1024)(128)(4,1)S(1)}, s32[]{:S(2)}) async-start(s8[9437184]{0:T(1024)(128)(4,1)} %bitcast.267), calls=%async_computation.30 | async-start | bytes 8388608
  379.9 17.6 %slice-start.2 = ((s8[9437184]{0:T(1024)(128)(4,1)}), s8[1048576]{0:T(1024)(128)(4,1)S(1)}, s32[]{:S(2)}) async-start(s8[9437184]{0:T(1024)(128)(4,1)} %bitcast.267), calls=%async_computation.31 | async-start | bytes 2097152
  405.8 10.7 all-to-all-start.4
  409.3 167.2 %reduce-scatter.10.cloned.1.call-start = ((), (), s32[]{:S(2)}) async-start(), calls=%async_computation.22 | async-start | bytes 1114112 | tf_op jit(solution)/shard_map/reduce_scatter | solution.py:339
  482.8 3.6 collective-permute-start.18
  485.6 26.0 %copy-start.33 = (f32[192,32]{0,1:T(8,128)S(1)}, f32[192,32]{0,1:T(8,128)}, u32[]{:S(2)}) copy-start(f32[192,32]{0,1:T(8,128)} %copy-done.32) | copy-start | bytes 73732
  485.6 26.0 %copy-start.35 = (f32[192,32]{0,1:T(8,128)S(1)}, f32[192,32]{0,1:T(8,128)}, u32[]{:S(2)}) copy-start(f32[192,32]{0,1:T(8,128)} %copy-done.34) | copy-start | bytes 73732
  486.5 25.3 %copy-start.18 = (f32[192,512]{0,1:T(8,128)S(1)}, f32[192,512]{0,1:T(8,128)}, u32[]{:S(2)}) copy-start(f32[192,512]{0,1:T(8,128)} %copy-done.17) | copy-start | bytes 1179652
  486.5 25.3 %copy-start.42 = (f32[192,8]{0,1:T(8,128)S(1)}, f32[192,8]{0,1:T(8,128)}, u32[]{:S(2)}) copy-start(f32[192,8]{0,1:T(8,128)} %copy-done.41) | copy-start | bytes 18436
  486.5 25.3 %copy-start.60 = (f32[64]{0:T(128)S(1)}, f32[64]{0:T(128)}, u32[]{:S(2)}) copy-start(f32[64]{0:T(128)} %copy-done.59) | copy-start | bytes 772
  486.5 8.2 collective-permute-start.19
  494.7 17.2 %copy-start.53 = (f32[192,8]{0,1:T(8,128)S(1)}, f32[192,8]{0,1:T(8,128)}, u32[]{:S(2)}) copy-start(f32[192,8]{0,1:T(8,128)} %copy-done.52) | copy-start | bytes 18436
  494.8 9.1 collective-permute-start.20
  514.4 122.5 %reduce-scatter.12.cloned.1.call-start = ((), (), s32[]{:S(2)}) async-start(), calls=%async_computation.23 | async-start | bytes 1114112 | tf_op jit(solution)/shard_map/reduce_scatter | solution.py:342
  523.5 177.7 %reduce-scatter.14.cloned.1.call-start = ((), (), s32[]{:S(2)}) async-start(), calls=%async_computation.24 | async-start | bytes 2228224 | tf_op jit(solution)/shard_map/reduce_scatter | solution.py:351
  525.7 240.2 %reduce-scatter.8.cloned.1.call-start = ((), (), s32[]{:S(2)}) async-start(), calls=%async_computation.21 | async-start | bytes 2228224 | tf_op jit(solution)/shard_map/reduce_scatter | solution.py:336
  539.9 340.5 %reduce-scatter.16.cloned.1.call-start = ((), (), s32[]{:S(2)}) async-start(), calls=%async_computation.25 | async-start | bytes 10027008 | tf_op jit(solution)/shard_map/reduce_scatter | solution.py:357
  546.8 449.2 %reduce-scatter.18.cloned.1.call-start = ((), (), s32[]{:S(2)}) async-start(), calls=%async_computation.26 | async-start | bytes 10027008 | tf_op jit(solution)/shard_map/reduce_scatter | solution.py:360
  553.4 557.8 %reduce-scatter.20.cloned.1.call-start = ((), (), s32[]{:S(2)}) async-start(), calls=%async_computation.27 | async-start | bytes 10027008 | tf_op jit(solution)/shard_map/reduce_scatter | solution.py:363
  561.0 550.3 %copy-start.13 = (f32[192,1024]{1,0:T(8,128)S(1)}, f32[192,1024]{1,0:T(8,128)}, u32[]{:S(2)}) copy-start(f32[192,1024]{1,0:T(8,128)} %copy-done.12) | copy-start | bytes 2359300
  561.0 618.4 %all-reduce.18.cloned.1.call-start = ((), (), s32[]{:S(2)}) async-start(), calls=%async_computation.28 | async-start | bytes 4325376 | tf_op jit(solution)/shard_map/psum | solution.py:369
  (64 other events, 380.4 us)
Sparse Core Ops, SparseCore 0:
  10.2 46.6 all-gather.8
  59.0 38.3 all-gather.10
  99.6 57.5 all-gather.6
  159.2 49.3 all-gather.12
  210.7 79.7 all-gather.14
  292.7 79.5 all-gather.16
  514.6 61.8 reduce-scatter.9
  580.5 56.3 reduce-scatter.11
  640.7 60.4 reduce-scatter.13
  705.3 60.5 reduce-scatter.7
  770.0 110.3 reduce-scatter.15
  884.9 111.1 reduce-scatter.17
  1000.1 111.0 reduce-scatter.19
  1114.1 65.2 all-reduce.17
